TPU v7x, 512 devices: a whole 4x4x16 slice. The times are simulated.
512 devices in a mesh: ep: 16 (over z), mx: 4 (over x), my: 8 (over y, core).
Axes of the slice: x: 4, y: 4, z: 16, core: 2. Of those that a mesh axis runs over, the one named last changes fastest.
Arguments:
- context: bfloat16 [16384, 2048], P(('ep', 'mx')), may hold values from -6 to 6
- resid_in: bfloat16 [16384, 2048], P(('ep', 'mx'), 'my'), may hold values from -70 to 70
- out_weight: bfloat16 [2048, 2048], P(None, 'my'), may hold values from -0.125 to 0.125
- norm_gain: float32 [2048], P('my'), may hold values from 0.5 to 1.5
- gate_weight: bfloat16 [8, 5632, 2048], P(None, ('ep', 'my'), 'mx'), may hold values from -0.125 to 0.125
- up_weight: bfloat16 [8, 5632, 2048], P(None, ('ep', 'my'), 'mx'), may hold values from -0.125 to 0.125
- down_weight: bfloat16 [8, 5632, 2048], P(None, ('ep', 'my'), 'mx'), may hold values from -0.078125 to 0.078125
- routes: int32 [16384, 2], P(('ep', 'mx')), may hold values from 0 to 7, all different within a row; in each aligned block of 256 rows (0 to 255, 256 to 511, ...) at most 96 rows name the same one
- gate_probs: float32 [16384, 2], P(('ep', 'mx')), may hold values from 0.05 to 1
- final_gain: float32 [2048], P('my'), may hold values from 0.5 to 1.5
Outputs:
- normed_out: bfloat16 [16384, 2048], P(('ep', 'mx'), 'my')
- stream_out: bfloat16 [16384, 2048], P(('ep', 'mx'), 'my')
Inputs may be any that keep to these rules, and one draw needn't show every extreme that they name: `routes`: each row names 2 different experts; in each aligned block of 256 rows no expert is named by more than 96 rows, a bound that some block reaches.
All inputs are finite; a program needn't handle non-finite values.
Results may differ from a plain program's by a relative error of at most 0.012.
Values may be sent and summed in bfloat16 or wider, within the bound.
A program may use at most 128 MiB of HBM per device.

v0:
```python
import jax
import jax.numpy as jnp
import numpy as np
from jax import lax
from jax.sharding import PartitionSpec as P

D = 2048
EXPERTS = 8
TOPK = 2
MOST = 96
EPSILON = 1e-06


def row_scale(stream_f):
    partial_sq = jnp.sum(stream_f * stream_f, axis=1)
    row_total = lax.psum(partial_sq, "my")
    return lax.rsqrt(row_total / D + EPSILON)


def shards(
    context,
    resid_in,
    out_weight,
    norm_gain,
    gate_weight,
    up_weight,
    down_weight,
    routes,
    gate_probs,
    final_gain,
):
    ep_count = lax.axis_size("ep")
    mx_count = lax.axis_size("mx")
    slot_dev = max(1, EXPERTS // ep_count)
    slot_total = slot_dev * ep_count
    replicas = slot_total // EXPERTS
    capacity = MOST // replicas
    tok_rows = context.shape[0]
    feat_block = resid_in.shape[1]
    piece_units = gate_weight.shape[1]
    width_block = gate_weight.shape[2]
    slot_rows = ep_count * capacity
    projected = jnp.dot(context, out_weight, preferred_element_type=jnp.float32)
    stream = (projected + resid_in.astype(jnp.float32)).astype(jnp.bfloat16)
    stream_f = stream.astype(jnp.float32)
    normed = (stream_f * row_scale(stream_f)[:, None] * norm_gain[None, :]).astype(jnp.bfloat16)
    chosen = routes.reshape(-1)
    onehot = (chosen[:, None] == jnp.arange(EXPERTS, dtype=jnp.int32)[None, :]).astype(jnp.int32)
    before = jnp.cumsum(onehot, axis=0) - onehot
    ranking = jnp.sum(before * onehot, axis=1)
    slot_index = chosen * replicas + ranking % replicas
    target = slot_index * capacity + ranking // replicas
    row_ids = jnp.arange(tok_rows * TOPK, dtype=jnp.int32) // TOPK
    source = jnp.full((slot_total * capacity,), tok_rows, jnp.int32).at[target].set(row_ids)
    padded = jnp.concatenate([normed, jnp.zeros((1, feat_block), jnp.bfloat16)], axis=0)
    packed = padded[source].reshape(ep_count, slot_dev, capacity, feat_block)
    landed = lax.all_to_all(packed, "ep", split_axis=0, concat_axis=0, tiled=True)
    gathered = lax.all_gather(landed, "my", axis=3, tiled=True)
    tokens_in = jnp.transpose(gathered, (1, 0, 2, 3)).reshape(slot_dev, slot_rows, D)
    split_rows = tokens_in.reshape(slot_dev, slot_rows, mx_count, width_block)
    expert_table = (
        np.arange(ep_count)[:, None] * slot_dev + np.arange(slot_dev)[None, :]
    ) // replicas

    def widen_pieces(weight):
        chosen_rows = weight[expert_table]
        wide = jnp.broadcast_to(
            chosen_rows[:, None], (ep_count, mx_count, slot_dev, piece_units, width_block)
        )
        return wide.reshape(ep_count * mx_count, slot_dev, piece_units, width_block)

    got_gate, got_up, got_down = (
        lax.all_to_all(
            widen_pieces(gate_weight), ("ep", "mx"), split_axis=0, concat_axis=0, tiled=True
        ),
        lax.all_to_all(
            widen_pieces(up_weight), ("ep", "mx"), split_axis=0, concat_axis=0, tiled=True
        ),
        lax.all_to_all(
            widen_pieces(down_weight), ("ep", "mx"), split_axis=0, concat_axis=0, tiled=True
        ),
    )
    dims_five = (ep_count, mx_count, slot_dev, piece_units, width_block)
    gate_proj = jnp.einsum(
        "jrad,sajfd->jrsf",
        split_rows,
        got_gate.reshape(dims_five),
        preferred_element_type=jnp.float32,
    )
    up_proj = jnp.einsum(
        "jrad,sajfd->jrsf",
        split_rows,
        got_up.reshape(dims_five),
        preferred_element_type=jnp.float32,
    )
    hidden = (jax.nn.silu(gate_proj) * up_proj).astype(jnp.bfloat16)
    expert_out = jnp.einsum(
        "jrsf,sajfd->jrad", hidden, got_down.reshape(dims_five), preferred_element_type=jnp.float32
    )
    expert_out = expert_out.reshape(slot_dev, slot_rows, D)
    summed = lax.psum_scatter(
        expert_out.astype(jnp.bfloat16), "my", scatter_dimension=2, tiled=True
    )
    sent_back = summed.reshape(slot_dev, ep_count, capacity, feat_block)
    sent_back = jnp.transpose(sent_back, (1, 0, 2, 3))
    returned = lax.all_to_all(sent_back, "ep", split_axis=0, concat_axis=0, tiled=True).reshape(
        slot_total * capacity, feat_block
    )
    picked = returned[target].reshape(tok_rows, TOPK, feat_block).astype(jnp.float32)
    weights_norm = gate_probs / jnp.sum(gate_probs, axis=1, keepdims=True)
    mixed = jnp.sum(weights_norm[:, :, None] * picked, axis=1)
    updated = stream_f + mixed
    normed_out = (updated * row_scale(updated)[:, None] * final_gain[None, :]).astype(jnp.bfloat16)
    return (normed_out, updated.astype(jnp.bfloat16))


def solution(mesh):
    placed = (
        P(("ep", "mx"), None),
        P(("ep", "mx"), "my"),
        P(None, "my"),
        P("my"),
        P(None, ("ep", "my"), "mx"),
        P(None, ("ep", "my"), "mx"),
        P(None, ("ep", "my"), "mx"),
        P(("ep", "mx"), None),
        P(("ep", "mx"), None),
        P("my"),
    )
    return jax.shard_map(
        shards,
        mesh=mesh,
        in_specs=placed,
        out_specs=(P(("ep", "mx"), "my"), P(("ep", "mx"), "my")),
        check_vma=False,
    )
```

profile of v0, /device:TPU:4, one launch (start us, length us, event | category | flops | bytes accessed | tf_op | source)
XLA Modules:
  0.0 643.5 jit_solution(12226968780941671538)
XLA Ops:
  10.9 2.4 scatter_custom_fusion
  15.2 14.9 %psum.14 = f32[256]{0:T(256)S(1)} all-reduce(f32[256]{0:T(256)S(1)} %get-tuple-element.4), channel_id=1, replica_groups=mesh['ep'=16,'mx'=4,'my'=8] {'my'}, use_global_device_ids=true, to_apply=%region_2.0 | all-reduce | flops 256 | bytes 2048 | tf_op jit(solution)/shard_map/psum | solution.py:16
  30.2 3.3 gather_fusion
  33.5 15.2 %all-to-all-start = ((bf16[16,1,48,256]{3,2,1,0:T(8,128)(2,1)}), bf16[16,1,48,256]{3,2,1,0:T(8,128)(2,1)}, u32[]{:S(2)}, u32[]{:S(2)}) async-start(bf16[16,1,48,256]{3,2,1,0:T(8,128)(2,1)} %bitcast.5), calls=%async_computation | async-start | bytes 786432 | tf_op jit(solution)/shard_map/all_to_all | solution.py:57
  48.8 2.6 gather_fusion.1
  51.8 18.0 %all-to-all-done = bf16[16,1,48,256]{3,2,1,0:T(8,128)(2,1)} async-done(((bf16[16,1,48,256]{3,2,1,0:T(8,128)(2,1)}), bf16[16,1,48,256]{3,2,1,0:T(8,128)(2,1)}, u32[]{:S(2)}, u32[]{:S(2)}) %all-to-all-start) | async-done | bytes 393248 | tf_op jit(solution)/shard_map/all_to_all | solution.py:57
  71.9 10.2 %all-to-all-start.1 = ((bf16[64,1,44,512]{3,2,1,0:T(8,128)(2,1)}), bf16[64,1,44,512]{3,2,1,0:T(8,128)(2,1)}, u32[]{:S(2)}, u32[]{:S(2)}) async-start(bf16[64,1,44,512]{3,2,1,0:T(8,128)(2,1)} %bitcast.87), calls=%async_computation.1 | async-start | bytes 6291456 | tf_op jit(solution)/shard_map/all_to_all | solution.py:73
  82.2 2.6 gather_fusion.3
  85.2 140.9 %all-to-all-done.1 = bf16[64,1,44,512]{3,2,1,0:T(8,128)(2,1)} async-done(((bf16[64,1,44,512]{3,2,1,0:T(8,128)(2,1)}), bf16[64,1,44,512]{3,2,1,0:T(8,128)(2,1)}, u32[]{:S(2)}, u32[]{:S(2)}) %all-to-all-start.1) | async-done | bytes 2883616 | tf_op jit(solution)/shard_map/all_to_all | solution.py:73
  228.2 6.3 all-to-all-start.3
  234.5 2.6 gather_fusion.2
  237.6 140.7 %all-to-all-done.3 = bf16[64,1,44,512]{3,2,1,0:T(8,128)(2,1)} async-done(((bf16[64,1,44,512]{3,2,1,0:T(8,128)(2,1)}), bf16[64,1,44,512]{3,2,1,0:T(8,128)(2,1)}, u32[]{:S(2)}, u32[]{:S(2)}) %all-to-all-start.3) | async-done | bytes 2883616 | tf_op jit(solution)/shard_map/all_to_all | solution.py:79
  380.4 6.1 all-to-all-start.2
  387.3 43.5 %all-gather.2.cloned.1.call-done = bf16[16,1,48,2048]{3,2,1,0:T(8,128)(2,1)} async-done(((bf16[16,1,48,256]{3,2,1,0:T(8,128)(2,1)}), bf16[16,1,48,2048]{3,2,1,0:T(8,128)(2,1)}) %all-gather.2.cloned.1.call-update) | async-done | bytes 3145744 | tf_op jit(solution)/shard_map/all_gather | solution.py:58
  430.8 6.2 reshape.196
  436.9 5.7 copy.61
  442.6 6.7 %dot_general.20 = bf16[2048,44,16]{0,2,1:T(8,128)(2,1)} reshape(bf16[4,512,44,16]{1,0,3,2:T(4,128)(2,1)} %bitcast.88) | data formatting | bytes 5767168 | tf_op jit(solution)/shard_map/jrsf,sajfd->jrad/dot_general | solution.py:97
  449.3 6.9 %fusion.2 = f32[768,16,44,1]{0,2,3,1:T(8,128)} fusion(bf16[768,4,512]{2,1,0:T(4,128)(2,1)} %reshape.196, bf16[16,4,44,512]{3,2,1,0:T(8,128)(2,1)} %bitcast.80), kind=kOutput, calls=%fused_computation.9 | convolution fusion | flops 2214592512 | bytes 8192000 | tf_op jit(solution)/shard_map/jrad,sajfd->jrsf/dot_general | solution.py:84
  456.2 73.2 %all-to-all-done.2 = bf16[64,1,44,512]{3,2,1,0:T(8,128)(2,1)} async-done(((bf16[64,1,44,512]{3,2,1,0:T(8,128)(2,1)}), bf16[64,1,44,512]{3,2,1,0:T(8,128)(2,1)}, u32[]{:S(2)}, u32[]{:S(2)}) %all-to-all-start.2) | async-done | bytes 2883616 | tf_op jit(solution)/shard_map/all_to_all | solution.py:76
  529.4 16.1 %fusion.7 = bf16[1,768,2048]{2,1,0:T(8,128)(2,1)} fusion(bf16[2048,44,16]{0,2,1:T(8,128)(2,1)} %dot_general.20, f32[768,16,44,1]{0,2,3,1:T(8,128)} %fusion.2, bf16[768,4,512]{2,1,0:T(4,128)(2,1)} %reshape.196, bf16[16,4,44,512]{3,2,1,0:T(8,128)(2,1)} %bitcast.83), kind=kOutput, calls=%fused_computation.14 | convolution fusion | flops 4434001920 | bytes 14221312 | tf_op jit(solution)/shard_map/jrsf,sajfd->jrad/dot_general | solution.py:97
  545.6 37.8 %reduce-scatter.2.cloned.1.call-done = bf16[1,768,256]{2,1,0:T(8,128)(2,1)} async-done(((bf16[1,768,2048]{2,1,0:T(8,128)(2,1)}), bf16[1,768,256]{2,1,0:T(8,128)(2,1)}) %reduce-scatter.2.cloned.1.call-update) | async-done | bytes 393232 | tf_op jit(solution)/shard_map/reduce_scatter | solution.py:101
  583.4 12.4 %all-to-all-start.4 = ((bf16[16,1,48,256]{3,2,1,0:T(8,128)(2,1)}), bf16[16,1,48,256]{3,2,1,0:T(8,128)(2,1)S(1)}, u32[]{:S(2)}, u32[]{:S(2)}) async-start(bf16[16,1,48,256]{3,2,1,0:T(8,128)(2,1)} %bitcast.89), calls=%async_computation.5 | async-start | bytes 786432 | tf_op jit(solution)/shard_map/all_to_all | solution.py:106
  596.0 20.1 %all-to-all-done.4 = bf16[16,1,48,256]{3,2,1,0:T(8,128)(2,1)S(1)} async-done(((bf16[16,1,48,256]{3,2,1,0:T(8,128)(2,1)}), bf16[16,1,48,256]{3,2,1,0:T(8,128)(2,1)S(1)}, u32[]{:S(2)}, u32[]{:S(2)}) %all-to-all-start.4) | async-done | bytes 393248 | tf_op jit(solution)/shard_map/all_to_all | solution.py:106
  619.8 16.1 %psum.15 = f32[256]{0:T(256)S(1)} all-reduce(f32[256]{0:T(256)S(1)} %multiply_reduce_fusion.1), channel_id=1, replica_groups=mesh['ep'=16,'mx'=4,'my'=8] {'my'}, use_global_device_ids=true, to_apply=%region_10.11 | all-reduce | flops 256 | bytes 2048 | tf_op jit(solution)/shard_map/psum | solution.py:16
  (58 shorter events, 18.6 us)
Async XLA Ops:
  7.2 6.2 copy-start
  7.2 22.9 %copy-start.5 = (f32[256]{0:T(256)S(1)}, f32[256]{0:T(256)}, u32[]{:S(2)}) copy-start(f32[256]{0:T(256)} %param.17) | copy-start | bytes 3076
  13.4 35.4 %copy-start.7 = (s32[16]{0:T(128)S(1)}, s32[16]{0:T(128)}, u32[]{:S(2)}) copy-start(s32[16]{0:T(128)} %constant.78) | copy-start | bytes 196
  13.4 35.4 %copy-start.1 = (bf16[8,44,512]{2,0,1:T(8,128)(2,1)S(1)}, bf16[8,44,512]{2,0,1:T(8,128)(2,1)}, u32[]{:S(2)}) copy-start(bf16[8,44,512]{2,0,1:T(8,128)(2,1)} %param.18) | copy-start | bytes 1081348
  33.5 36.3 %all-to-all-start = ((bf16[16,1,48,256]{3,2,1,0:T(8,128)(2,1)}), bf16[16,1,48,256]{3,2,1,0:T(8,128)(2,1)}, u32[]{:S(2)}, u32[]{:S(2)}) async-start(bf16[16,1,48,256]{3,2,1,0:T(8,128)(2,1)} %bitcast.5), calls=%async_computation | async-start | bytes 786432 | tf_op jit(solution)/shard_map/all_to_all | solution.py:57
  71.9 10.3 %copy-start.2 = (bf16[8,44,512]{2,0,1:T(8,128)(2,1)S(1)}, bf16[8,44,512]{2,0,1:T(8,128)(2,1)}, u32[]{:S(2)}) copy-start(bf16[8,44,512]{2,0,1:T(8,128)(2,1)} %param.20) | copy-start | bytes 1081348
  71.9 154.2 %all-to-all-start.1 = ((bf16[64,1,44,512]{3,2,1,0:T(8,128)(2,1)}), bf16[64,1,44,512]{3,2,1,0:T(8,128)(2,1)}, u32[]{:S(2)}, u32[]{:S(2)}) async-start(bf16[64,1,44,512]{3,2,1,0:T(8,128)(2,1)} %bitcast.87), calls=%async_computation.1 | async-start | bytes 6291456 | tf_op jit(solution)/shard_map/all_to_all | solution.py:73
  228.2 6.3 copy-start.3
  228.2 150.0 %all-to-all-start.3 = ((bf16[64,1,44,512]{3,2,1,0:T(8,128)(2,1)}), bf16[64,1,44,512]{3,2,1,0:T(8,128)(2,1)}, u32[]{:S(2)}, u32[]{:S(2)}) async-start(bf16[64,1,44,512]{3,2,1,0:T(8,128)(2,1)} %bitcast.86), calls=%async_computation.3 | async-start | bytes 6291456 | tf_op jit(solution)/shard_map/all_to_all | solution.py:79
  380.4 149.0 %all-to-all-start.2 = ((bf16[64,1,44,512]{3,2,1,0:T(8,128)(2,1)}), bf16[64,1,44,512]{3,2,1,0:T(8,128)(2,1)}, u32[]{:S(2)}, u32[]{:S(2)}) async-start(bf16[64,1,44,512]{3,2,1,0:T(8,128)(2,1)} %bitcast.85), calls=%async_computation.2 | async-start | bytes 6291456 | tf_op jit(solution)/shard_map/all_to_all | solution.py:76
  386.5 44.3 %all-gather.2.cloned.1.call-start = ((), (), s32[]{:S(2)}) async-start(), calls=%async_computation.6 | async-start | bytes 3538944 | tf_op jit(solution)/shard_map/all_gather | solution.py:58
  387.3 196.1 %reduce-scatter.2.cloned.1.call-start = ((), (), s32[]{:S(2)}) async-start(), calls=%async_computation.7 | async-start | bytes 3538944 | tf_op jit(solution)/shard_map/reduce_scatter | solution.py:101
  545.5 50.3 %copy-start.4 = (f32[256,2]{0,1:T(2,128)S(1)}, f32[256,2]{0,1:T(2,128)}, u32[]{:S(2)}) copy-start(f32[256,2]{0,1:T(2,128)} %param.22) | copy-start | bytes 6148
  545.6 90.4 %copy-start.6 = (f32[256]{0:T(256)S(1)}, f32[256]{0:T(256)}, u32[]{:S(2)}) copy-start(f32[256]{0:T(256)} %param.23) | copy-start | bytes 3076
  583.4 32.7 %all-to-all-start.4 = ((bf16[16,1,48,256]{3,2,1,0:T(8,128)(2,1)}), bf16[16,1,48,256]{3,2,1,0:T(8,128)(2,1)S(1)}, u32[]{:S(2)}, u32[]{:S(2)}) async-start(bf16[16,1,48,256]{3,2,1,0:T(8,128)(2,1)} %bitcast.89), calls=%async_computation.5 | async-start | bytes 786432 | tf_op jit(solution)/shard_map/all_to_all | solution.py:106
Sparse Core Ops, SparseCore 0:
  389.5 41.2 all-gather.1
  545.7 37.6 reduce-scatter.1
where the time goes:
time: 644 us
  waiting for transfers between devices  475 us (74%)
  starting transfers between devices  50.4 us (8%)
  local copies, waits for them, and re-layouts  43.7 us (7%)
  blocking collectives  31 us (5%)
  matrix products  24.8 us (4%)
  between operations  14.3 us (2%)
    all_to_all x1, waiting for transfers between devices, shards(): lax.all_to_all(widen_pieces(gate_weight), ('ep', 'mx'), split_axis=0, con...  141 us
    all_to_all x1, waiting for transfers between devices, shards(): lax.all_to_all(widen_pieces(down_weight), ('ep', 'mx'), split_axis=0, con...  141 us
    all_to_all x1, waiting for transfers between devices, shards(): lax.all_to_all(widen_pieces(up_weight), ('ep', 'mx'), split_axis=0, conca...  73.2 us
    all_gather x1, waiting for transfers between devices, shards(): gathered = lax.all_gather(landed, 'my', axis=3, tiled=True)  43.5 us
    reduce_scatter x1, waiting for transfers between devices, shards(): lax.psum_scatter(expert_out.astype(jnp.bfloat16), 'my', scatter_dimension...  37.8 us
    psum x2, blocking collectives, row_scale(): row_total = lax.psum(partial_sq, 'my')  31 us
    all_to_all x1, waiting for transfers between devices, shards(): lax.all_to_all(sent_back, 'ep', split_axis=0, concat_axis=0, tiled=True)  20.1 us
    all_to_all x1, waiting for transfers between devices, shards(): lax.all_to_all(packed, 'ep', split_axis=0, concat_axis=0, tiled=True)  18 us
  transfers between devices with their start and end apart: 7, of which 7 were waited for; matrix products, arithmetic and copies ran while one was open for 5% of the time, Pallas kernels for 0%

commit v1 on v0

--- a/solution.py
+++ b/solution.py
@@ -29,6 +29,12 @@
     gate_probs,
     final_gain,
 ):
+
+    def _tell_side(arr_in):
+        return jnp.concatenate(
+            lax.all_to_all(jnp.stack([arr_in] * lax.psum(1, "my"), axis=0), "my", 0, 0), axis=3
+        )
+
     ep_count = lax.axis_size("ep")
     mx_count = lax.axis_size("mx")
     slot_dev = max(1, EXPERTS // ep_count)
@@ -55,7 +61,7 @@
     padded = jnp.concatenate([normed, jnp.zeros((1, feat_block), jnp.bfloat16)], axis=0)
     packed = padded[source].reshape(ep_count, slot_dev, capacity, feat_block)
     landed = lax.all_to_all(packed, "ep", split_axis=0, concat_axis=0, tiled=True)
-    gathered = lax.all_gather(landed, "my", axis=3, tiled=True)
+    gathered = _tell_side(landed)
     tokens_in = jnp.transpose(gathered, (1, 0, 2, 3)).reshape(slot_dev, slot_rows, D)
     split_rows = tokens_in.reshape(slot_dev, slot_rows, mx_count, width_block)
     expert_table = (

time: 644 us -> 687 us (1.067)
  the two profiles are of different devices: /device:TPU:4 before, /device:TPU:2 now
where the time goes in v1:
time: 687 us; the launch traced here: 686 us
  waiting for transfers between devices  486 us (71%)
  blocking collectives  66.9 us (10%)
  local copies, waits for them, and re-layouts  50.1 us (7%)
  starting transfers between devices  39.4 us (6%)
  matrix products  24.8 us (4%)
  between operations  14.3 us (2%)
    all_to_all x1, waiting for transfers between devices, shards(): lax.all_to_all(widen_pieces(gate_weight), ('ep', 'mx'), split_axis=0, con...  142 us
    all_to_all x1, waiting for transfers between devices, shards(): lax.all_to_all(widen_pieces(down_weight), ('ep', 'mx'), split_axis=0, con...  141 us
    all_to_all x1, waiting for transfers between devices, shards(): lax.all_to_all(widen_pieces(up_weight), ('ep', 'mx'), split_axis=0, conca...  114 us
    all_to_all x1, blocking collectives, shards(): lax.all_to_all(packed, 'ep', split_axis=0, concat_axis=0, tiled=True)  36 us
    all_to_all x1, waiting for transfers between devices, _tell_side(): lax.all_to_all(jnp.stack([arr_in] * lax.psum(1, 'my'), axis=0), 'my', 0, 0)  35.5 us
    reduce_scatter x1, waiting for transfers between devices, shards(): lax.psum_scatter(expert_out.astype(jnp.bfloat16), 'my', scatter_dimension...  33.3 us
    psum x2, blocking collectives, row_scale(): row_total = lax.psum(partial_sq, 'my')  30.9 us
    all_to_all x1, waiting for transfers between devices, shards(): lax.all_to_all(sent_back, 'ep', split_axis=0, concat_axis=0, tiled=True)  20.1 us
  transfers between devices with their start and end apart: 6, of which 6 were waited for; matrix products, arithmetic and copies ran while one was open for 6% of the time, Pallas kernels for 0%

profile of v1, /device:TPU:2, one launch (start us, length us, event | category | flops | bytes accessed | tf_op | source)
XLA Modules:
  0.0 685.6 jit_solution(5144222191437310215)
XLA Ops:
  15.1 14.9 %psum.14 = f32[256]{0:T(256)S(1)} all-reduce(f32[256]{0:T(256)S(1)} %get-tuple-element.4), channel_id=1, replica_groups=mesh['ep'=16,'mx'=4,'my'=8] {'my'}, use_global_device_ids=true, to_apply=%region_2.0 | all-reduce | flops 256 | bytes 2048 | tf_op jit(solution)/shard_map/psum | solution.py:16
  30.1 2.7 gather_fusion
  32.8 36.0 %all_to_all.33 = bf16[16,1,48,256]{3,2,1,0:T(8,128)(2,1)S(1)} all-to-all(bf16[16,1,48,256]{3,2,1,0:T(8,128)(2,1)S(1)} %bitcast.94), channel_id=1, replica_groups=mesh['ep'=16,'mx'=4,'my'=8] {'ep'}, dimensions={0} | all-to-all | bytes 786432 | tf_op jit(solution)/shard_map/all_to_all | solution.py:63
  70.7 5.7 all-to-all-start.1
  76.5 2.6 gather_fusion.1
  79.5 35.5 %all-to-all-done.1 = bf16[8,16,1,48,256]{4,3,1,2,0:T(8,128)(2,1)} async-done(((bf16[8,16,1,48,256]{4,3,1,2,0:T(8,128)(2,1)}), bf16[8,16,1,48,256]{4,3,1,2,0:T(8,128)(2,1)}, u32[]{:S(2)}, u32[]{:S(2)}) %all-to-all-start.1) | async-done | bytes 3145760 | tf_op jit(solution)/shard_map/all_to_all | solution.py:35
  117.1 9.0 %all-to-all-start.2 = ((bf16[64,1,44,512]{3,2,1,0:T(8,128)(2,1)}), bf16[64,1,44,512]{3,2,1,0:T(8,128)(2,1)}, u32[]{:S(2)}, u32[]{:S(2)}) async-start(bf16[64,1,44,512]{3,2,1,0:T(8,128)(2,1)} %bitcast.91), calls=%async_computation.2 | async-start | bytes 6291456 | tf_op jit(solution)/shard_map/all_to_all | solution.py:79
  126.1 2.6 gather_fusion.3
  129.2 141.8 %all-to-all-done.2 = bf16[64,1,44,512]{3,2,1,0:T(8,128)(2,1)} async-done(((bf16[64,1,44,512]{3,2,1,0:T(8,128)(2,1)}), bf16[64,1,44,512]{3,2,1,0:T(8,128)(2,1)}, u32[]{:S(2)}, u32[]{:S(2)}) %all-to-all-start.2) | async-done | bytes 2883616 | tf_op jit(solution)/shard_map/all_to_all | solution.py:79
  273.0 6.3 all-to-all-start.4
  279.3 2.6 gather_fusion.2
  282.3 141.3 %all-to-all-done.4 = bf16[64,1,44,512]{3,2,1,0:T(8,128)(2,1)} async-done(((bf16[64,1,44,512]{3,2,1,0:T(8,128)(2,1)}), bf16[64,1,44,512]{3,2,1,0:T(8,128)(2,1)}, u32[]{:S(2)}, u32[]{:S(2)}) %all-to-all-start.4) | async-done | bytes 2883616 | tf_op jit(solution)/shard_map/all_to_all | solution.py:85
  425.8 6.1 all-to-all-start.3
  431.9 5.3 copy.33
  437.3 6.0 reshape.203
  443.2 5.7 copy.62
  448.9 6.7 dot_general.20
  455.6 6.9 %fusion.2 = f32[768,16,44,1]{0,2,3,1:T(8,128)} fusion(bf16[768,4,512]{2,1,0:T(4,128)(2,1)} %reshape.203, bf16[16,4,44,512]{3,2,1,0:T(8,128)(2,1)} %bitcast.84), kind=kOutput, calls=%fused_computation.9 | convolution fusion | flops 2214592512 | bytes 8192000 | tf_op jit(solution)/shard_map/jrad,sajfd->jrsf/dot_general | solution.py:90
  462.5 113.7 %all-to-all-done.3 = bf16[64,1,44,512]{3,2,1,0:T(8,128)(2,1)} async-done(((bf16[64,1,44,512]{3,2,1,0:T(8,128)(2,1)}), bf16[64,1,44,512]{3,2,1,0:T(8,128)(2,1)}, u32[]{:S(2)}, u32[]{:S(2)}) %all-to-all-start.3) | async-done | bytes 2883616 | tf_op jit(solution)/shard_map/all_to_all | solution.py:82
  576.2 16.1 %fusion.7 = bf16[1,768,2048]{2,1,0:T(8,128)(2,1)} fusion(bf16[2048,44,16]{0,2,1:T(8,128)(2,1)} %dot_general.20, f32[768,16,44,1]{0,2,3,1:T(8,128)} %fusion.2, bf16[768,4,512]{2,1,0:T(4,128)(2,1)} %reshape.203, bf16[16,4,44,512]{3,2,1,0:T(8,128)(2,1)} %bitcast.87), kind=kOutput, calls=%fused_computation.14 | convolution fusion | flops 4434001920 | bytes 14221312 | tf_op jit(solution)/shard_map/jrsf,sajfd->jrad/dot_general | solution.py:103
  592.3 33.3 %reduce-scatter.2.cloned.1.call-done = bf16[1,768,256]{2,1,0:T(8,128)(2,1)} async-done(((bf16[1,768,2048]{2,1,0:T(8,128)(2,1)}), bf16[1,768,256]{2,1,0:T(8,128)(2,1)}) %reduce-scatter.2.cloned.1.call-update) | async-done | bytes 393232 | tf_op jit(solution)/shard_map/reduce_scatter | solution.py:107
  625.6 12.3 %all-to-all-start.5 = ((bf16[16,1,48,256]{3,2,1,0:T(8,128)(2,1)}), bf16[16,1,48,256]{3,2,1,0:T(8,128)(2,1)S(1)}, u32[]{:S(2)}, u32[]{:S(2)}) async-start(bf16[16,1,48,256]{3,2,1,0:T(8,128)(2,1)} %bitcast.95), calls=%async_computation.6 | async-start | bytes 786432 | tf_op jit(solution)/shard_map/all_to_all | solution.py:112
  638.1 20.1 %all-to-all-done.5 = bf16[16,1,48,256]{3,2,1,0:T(8,128)(2,1)S(1)} async-done(((bf16[16,1,48,256]{3,2,1,0:T(8,128)(2,1)}), bf16[16,1,48,256]{3,2,1,0:T(8,128)(2,1)S(1)}, u32[]{:S(2)}, u32[]{:S(2)}) %all-to-all-start.5) | async-done | bytes 393248 | tf_op jit(solution)/shard_map/all_to_all | solution.py:112
  662.0 16.0 %psum.15 = f32[256]{0:T(256)S(1)} all-reduce(f32[256]{0:T(256)S(1)} %multiply_reduce_fusion.1), channel_id=1, replica_groups=mesh['ep'=16,'mx'=4,'my'=8] {'my'}, use_global_device_ids=true, to_apply=%region_10.11 | all-reduce | flops 256 | bytes 2048 | tf_op jit(solution)/shard_map/psum | solution.py:16
  (58 shorter events, 22.2 us)
Async XLA Ops:
  7.2 6.2 copy-start
  7.2 22.8 %copy-start.5 = (f32[256]{0:T(256)S(1)}, f32[256]{0:T(256)}, u32[]{:S(2)}) copy-start(f32[256]{0:T(256)} %param.17) | copy-start | bytes 3076
  70.7 5.8 copy-start.7
  70.7 5.8 copy-start.1
  70.7 44.3 %all-to-all-start.1 = ((bf16[8,16,1,48,256]{4,3,1,2,0:T(8,128)(2,1)}), bf16[8,16,1,48,256]{4,3,1,2,0:T(8,128)(2,1)}, u32[]{:S(2)}, u32[]{:S(2)}) async-start(bf16[8,16,1,48,256]{4,3,1,2,0:T(8,128)(2,1)} %stack.2), calls=%async_computation.1 | async-start | bytes 6291456 | tf_op jit(solution)/shard_map/all_to_all | solution.py:35
  117.1 9.0 %copy-start.2 = (bf16[8,44,512]{2,0,1:T(8,128)(2,1)S(1)}, bf16[8,44,512]{2,0,1:T(8,128)(2,1)}, u32[]{:S(2)}) copy-start(bf16[8,44,512]{2,0,1:T(8,128)(2,1)} %param.20) | copy-start | bytes 1081348
  117.1 153.8 %all-to-all-start.2 = ((bf16[64,1,44,512]{3,2,1,0:T(8,128)(2,1)}), bf16[64,1,44,512]{3,2,1,0:T(8,128)(2,1)}, u32[]{:S(2)}, u32[]{:S(2)}) async-start(bf16[64,1,44,512]{3,2,1,0:T(8,128)(2,1)} %bitcast.91), calls=%async_computation.2 | async-start | bytes 6291456 | tf_op jit(solution)/shard_map/all_to_all | solution.py:79
  273.0 6.3 copy-start.3
  273.0 150.6 %all-to-all-start.4 = ((bf16[64,1,44,512]{3,2,1,0:T(8,128)(2,1)}), bf16[64,1,44,512]{3,2,1,0:T(8,128)(2,1)}, u32[]{:S(2)}, u32[]{:S(2)}) async-start(bf16[64,1,44,512]{3,2,1,0:T(8,128)(2,1)} %bitcast.90), calls=%async_computation.4 | async-start | bytes 6291456 | tf_op jit(solution)/shard_map/all_to_all | solution.py:85
  425.8 150.4 %all-to-all-start.3 = ((bf16[64,1,44,512]{3,2,1,0:T(8,128)(2,1)}), bf16[64,1,44,512]{3,2,1,0:T(8,128)(2,1)}, u32[]{:S(2)}, u32[]{:S(2)}) async-start(bf16[64,1,44,512]{3,2,1,0:T(8,128)(2,1)} %bitcast.89), calls=%async_computation.3 | async-start | bytes 6291456 | tf_op jit(solution)/shard_map/all_to_all | solution.py:82
  431.9 193.8 %reduce-scatter.2.cloned.1.call-start = ((), (), s32[]{:S(2)}) async-start(), calls=%async_computation.7 | async-start | bytes 3538944 | tf_op jit(solution)/shard_map/reduce_scatter | solution.py:107
  592.3 45.6 %copy-start.4 = (f32[256,2]{0,1:T(2,128)S(1)}, f32[256,2]{0,1:T(2,128)}, u32[]{:S(2)}) copy-start(f32[256,2]{0,1:T(2,128)} %param.22) | copy-start | bytes 6148
  592.3 85.7 %copy-start.6 = (f32[256]{0:T(256)S(1)}, f32[256]{0:T(256)}, u32[]{:S(2)}) copy-start(f32[256]{0:T(256)} %param.23) | copy-start | bytes 3076
  625.6 32.6 %all-to-all-start.5 = ((bf16[16,1,48,256]{3,2,1,0:T(8,128)(2,1)}), bf16[16,1,48,256]{3,2,1,0:T(8,128)(2,1)S(1)}, u32[]{:S(2)}, u32[]{:S(2)}) async-start(bf16[16,1,48,256]{3,2,1,0:T(8,128)(2,1)} %bitcast.95), calls=%async_computation.6 | async-start | bytes 786432 | tf_op jit(solution)/shard_map/all_to_all | solution.py:112
Sparse Core Ops, SparseCore 0:
  592.4 33.1 reduce-scatter.1
